TPU v7x, 32 devices: a whole 2x2x4 slice. The times are simulated.
32 devices in a mesh: grp: 2 (over y), tok: 16 (over z, x, core).
Axes of the slice: x: 2, y: 2, z: 4, core: 2. Of those that a mesh axis runs over, the one named last changes fastest.
Arguments:
- hidden: bfloat16 [4, 1024, 1536], P('grp', 'tok'), parts along dimension 0
- base_ids: int32 [4, 1024], P('grp', 'tok'), parts along dimension 0, may hold values from 0 to 4, as said below
- attn_gain: bfloat16 [1536], replicated, may hold values from 0.099609375 to 1.8984375
- q_weight: bfloat16 [1536, 768], replicated
- kv_weight: bfloat16 [1536, 384], replicated
- out_weight: bfloat16 [768, 1536], replicated, may hold values from -0.21875 to 0.21875
- head_gain: bfloat16 [1536], replicated, may hold values from 0.099609375 to 1.8984375
- head_weight: bfloat16 [1536, 1536], replicated, may hold values from -0.15625 to 0.15625
- head_bias: float32 [1536], replicated, may hold values from -1 to 1
- track_perm: int32 [1536], replicated, may hold values from 0 to 1535, each once
Outputs:
- combined: float32 [2048, 1536], P(('grp', 'tok')), parts along dimension 0
There are 2 independent parts, one for each index of `grp`. A program takes and returns all parts, laid end to end along the dimension named above; an argument that names none is the same for every part. Nothing has to cross between parts.
Inputs may be any that keep to these rules, and one draw needn't show every extreme that they name: `base_ids`: every eighth token of each strand, from token 0, has a base 0 to 3.
All inputs are finite; a program needn't handle non-finite values.
Results may differ from a plain program's by a relative error of at most 0.0058.
Values may be sent and summed in bfloat16 or wider, within the bound.
No kernel may reach another device: no remote copies, remote signals or barrier semaphores. Data moves between devices by JAX's collectives and lax.ppermute only.
A program may use at most 128 MiB of HBM per device.

v0:
```python
import math
import jax
import jax.numpy as jnp
from jax import lax
from jax.sharding import PartitionSpec as P


def swapped(value, axis, distance):
    mask = 2**distance
    pairs = [(source, source ^ mask) for source in range(lax.axis_size(axis))]
    return lax.ppermute(value, axis, pairs)


def normalize(rows, gain):
    widened = rows.astype(jnp.float32)
    return (
        widened
        * lax.rsqrt(jnp.mean(widened * widened, -1, keepdims=True) + 1e-06)
        * gain.astype(jnp.float32)
    )


def attend(running, queries, key_value, usable_flag):
    maxima, totals, accumulated = running
    width_head = queries.shape[2]
    key_rows = key_value[:, :, :width_head]
    value_rows = key_value[:, :, width_head:]
    scores = jnp.einsum("srd,skd->srk", queries, key_rows, preferred_element_type=jnp.float32) * (
        1.0 / math.sqrt(width_head)
    )
    usable = usable_flag[:, None, :] > 0
    scores = jnp.where(usable, scores, jnp.float32(-1e30))
    new_maxima = jnp.maximum(maxima, jnp.max(scores, -1))
    weight_exp = jnp.where(usable, jnp.exp(scores - new_maxima[:, :, None]), jnp.float32(0.0))
    totals = jnp.sum(weight_exp, -1)
    summed = jnp.einsum(
        "srk,skd->srd",
        weight_exp.astype(jnp.bfloat16),
        value_rows,
        preferred_element_type=jnp.float32,
    )
    accumulated = summed
    return (new_maxima, totals, accumulated)


def per_device(
    hidden,
    base_ids,
    attn_gain,
    q_weight,
    kv_weight,
    out_weight,
    head_gain,
    head_weight,
    head_bias,
    track_perm,
):
    tok_rows = hidden.shape[1]
    width_head = kv_weight.shape[1] // 2
    head_count = q_weight.shape[1] // width_head
    bit_count = lax.axis_size("tok").bit_length() - 1
    normed = normalize(hidden, attn_gain).astype(jnp.bfloat16)
    key_value = jnp.einsum(
        "std,de->ste", normed, kv_weight, preferred_element_type=jnp.float32
    ).astype(jnp.bfloat16)
    usable_flag = (base_ids != 4).astype(jnp.bfloat16)
    partner = hidden[1]
    for bit_number in range(bit_count):
        partner = swapped(partner, "tok", bit_number)
    partner = partner[::-1]
    query_source = jnp.stack([normed[0], normalize(partner, attn_gain).astype(jnp.bfloat16)])
    residual_base = jnp.stack([hidden[0], partner])
    queries = jnp.einsum(
        "std,de->ste", query_source, q_weight, preferred_element_type=jnp.float32
    ).astype(jnp.bfloat16)
    queries = queries.reshape(2, tok_rows * head_count, width_head)
    row_count = queries.shape[1]
    start_state = (
        jnp.full((2, row_count), -1e30, jnp.float32),
        jnp.zeros((2, row_count), jnp.float32),
        jnp.zeros((2, row_count, width_head), jnp.float32),
    )
    softmax_state = attend(
        start_state,
        queries,
        lax.all_gather(key_value, "tok", axis=1, tiled=True),
        lax.all_gather(usable_flag, "tok", axis=1, tiled=True),
    )
    maxima, totals, accumulated = softmax_state
    attended = (
        (accumulated / totals[:, :, None])
        .astype(jnp.bfloat16)
        .reshape(2, tok_rows, head_count * width_head)
    )
    residual_sum = residual_base.astype(jnp.float32) + jnp.einsum(
        "ste,ed->std", attended, out_weight, preferred_element_type=jnp.float32
    )
    normed_out = normalize(residual_sum, head_gain).astype(jnp.bfloat16)
    forward_logits = (
        jnp.dot(normed_out[0], head_weight, preferred_element_type=jnp.float32) + head_bias
    )
    reverse_logits = (
        jnp.dot(normed_out[1], head_weight[:, track_perm], preferred_element_type=jnp.float32)
        + head_bias[track_perm]
    )
    forward_pred = jax.nn.softplus(forward_logits).astype(jnp.bfloat16)
    reverse_pred = jax.nn.softplus(reverse_logits).astype(jnp.bfloat16)
    return 0.5 * (forward_pred.astype(jnp.float32) + reverse_pred.astype(jnp.float32))


def solution(mesh):
    placed = (P("grp", "tok", None), P("grp", "tok"), P(), P(), P(), P(), P(), P(), P(), P())
    return jax.shard_map(
        per_device, mesh=mesh, in_specs=placed, out_specs=P(("grp", "tok"), None), check_vma=False
    )
```

profile of v0, /device:TPU:0, one launch (start us, length us, event | category | flops | bytes accessed | tf_op | source)
XLA Modules:
  0.0 101.3 jit_solution(12420879725566651075)
XLA Ops:
  6.5 0.0 all-gather.3.cloned.1.call-start
  6.6 0.8 convert_element_type.55
  7.4 1.2 %fusion.25 = f32[2,64]{1,0:T(2,128)S(1)} fusion(bf16[2,64,1536]{2,1,0:T(8,128)(2,1)} %param.10), kind=kLoop, calls=%fused_computation.31 | loop fusion | flops 589696 | bytes 393728 | tf_op jit(solution)/shard_map/reduce_sum | solution.py:18
  8.6 1.2 %fusion.27 = bf16[2,64,1536]{2,1,0:T(8,128)(2,1)S(1)} fusion(bf16[2,64,1536]{2,1,0:T(8,128)(2,1)} %param.10, f32[1536]{0:T(1024)S(1)} %convert_element_type.55, f32[2,64]{1,0:T(2,128)S(1)} %add_rsqrt_fusion.1), kind=kLoop, calls=%fused_computation.33 | loop fusion | flops 786432 | bytes 793088 | tf_op jit(solution)/shard_map/convert_element_type | solution.py:62
  9.8 0.0 copy-start.3
  9.8 2.4 %fusion.13 = bf16[2,64,384]{2,1,0:T(8,128)(2,1)} fusion(bf16[2,64,1536]{2,1,0:T(8,128)(2,1)S(1)} %fusion.27, bf16[1536,384]{1,0:T(8,128)(2,1)} %param.14), kind=kOutput, calls=%fused_computation.20 | convolution fusion | flops 151044096 | bytes 1671168 | tf_op jit(solution)/shard_map/std,de->ste/dot_general | solution.py:63
  12.2 0.0 all-gather.3.cloned.1.call-update
  12.3 0.6 collective-permute-start
  12.8 1.1 %collective-permute-done = bf16[64,1536]{1,0:T(8,128)(2,1)S(1)} collective-permute-done((bf16[64,1536]{1,0:T(8,128)(2,1)S(1)}, bf16[64,1536]{1,0:T(8,128)(2,1)S(1)}, u32[]{:S(2)}, u32[]{:S(2)}) %collective-permute-start) | collective-permute-done | bytes 196640 | tf_op jit(solution)/shard_map/ppermute | solution.py:11
  13.9 2.8 %collective-permute-start.1 = (bf16[64,1536]{1,0:T(8,128)(2,1)S(1)}, bf16[64,1536]{1,0:T(8,128)(2,1)S(1)}, u32[]{:S(2)}, u32[]{:S(2)}) collective-permute-start(bf16[64,1536]{1,0:T(8,128)(2,1)S(1)} %collective-permute-done), channel_id=1, source_target_pairs={{0,2},{1,3},{2,0},{3,1},{4,6},{5,7},{6,4},{7,5},{8,10},{9,11},{10,... | collective-permute-start | bytes 589832 | tf_op jit(solution)/shard_map/ppermute | solution.py:11
  16.7 20.7 %all-gather = bf16[16,64,2]{1,2,0:T(2,128)(2,1)S(1)} all-gather(bf16[1,64,2]{1,2,0:T(2,128)(2,1)S(1)} %fusion.37), channel_id=1, replica_groups=mesh['grp'=2,'tok'=16] {'tok'}, dimensions={0}, use_global_device_ids=true | all-gather | bytes 4352 | tf_op jit(solution)/shard_map/all_gather | solution.py:87
  37.4 11.5 %collective-permute-done.2 = bf16[64,1536]{1,0:T(8,128)(2,1)} collective-permute-done((bf16[64,1536]{1,0:T(8,128)(2,1)S(1)}, bf16[64,1536]{1,0:T(8,128)(2,1)}, u32[]{:S(2)}, u32[]{:S(2)}) %collective-permute-start.2) | collective-permute-done | bytes 196640 | tf_op jit(solution)/shard_map/ppermute | solution.py:11
  48.9 0.0 copy-start.5
  48.9 6.7 %copy.26 = bf16[1536,1536]{0,1:T(8,128)(2,1)} copy(bf16[1536,1536]{1,0:T(8,128)(2,1)} %param.17) | data formatting | bytes 9437184 | tf_op args[7]
  55.7 0.1 reshape.64
  55.8 0.0 copy-start.1
  55.8 13.4 %gather_fusion = bf16[1536,1536]{1,0:T(8,128)(2,1)} fusion(bf16[1536,1536]{0,1:T(8,128)(2,1)} %copy.26, s32[2048]{0:T(1024)S(1)} %pad_clamp_fusion), kind=kCustom, calls=%fused_computation | custom fusion | bytes 9443328 | tf_op jit(solution)/shard_map/gather | solution.py:103
  69.2 8.4 %gather_fusion.1 = f32[1536]{0:T(1024)S(1)} fusion(f32[1536]{0:T(1024)S(1)} %copy-done.1, s32[2048]{0:T(1024)S(1)} %pad_clamp_fusion), kind=kCustom, calls=%fused_computation.1 | custom fusion | bytes 18432 | tf_op jit(solution)/shard_map/gather | solution.py:104
  77.6 0.3 rev.3
  77.9 0.1 fusion.28
  78.1 0.1 fusion.36
  78.2 2.2 %fusion.10 = bf16[2,64,768]{2,1,0:T(8,128)(2,1)S(1)} fusion(bf16[1536,768]{1,0:T(8,128)(2,1)} %param.13, bf16[1,64,1536]{2,1,0:T(8,128)(2,1)S(1)} %fusion.36, bf16[1,64,1536]{2,1,0:T(8,128)(2,1)S(1)} %slice-done), kind=kOutput, calls=%fused_computation.19 | convolution fusion | flops 302284800 | bytes 2949120 | tf_op jit(solution)/shard_map/std,de->ste/dot_general | solution.py:73
  80.4 1.0 reshape.41
  81.3 2.0 %fusion.4 = (f32[2,256]{1,0:T(2,128)S(1)}, f32[2,256,1024]{2,1,0:T(8,128)S(1)}) fusion(pred[2,1024]{1,0:T(4,128)(4,1)S(1)} %bitcast.40, bf16[2,256,192]{2,1,0:T(8,128)(2,1)} %reshape.41, bf16[2,1024,384]{2,1,0:T(8,128)(2,1)} %all-gather.3.cloned.1.call-done), kind=kOutput, calls=%fused_computation.10 | convolution fusion | flops 202898944 | bytes 3411968 | tf_op jit(solution)/shard_map/srd,skd->srk/dot_general | solution.py:28
  83.4 0.6 fusion.5
  84.0 1.2 %fusion.9 = bf16[2,256,192]{1,2,0:T(8,128)(2,1)S(1)} fusion(f32[2,256,1024]{2,1,0:T(8,128)S(1)} %get-tuple-element.8, bf16[2,1024,384]{2,1,0:T(8,128)(2,1)S(1)} %copy-done.6, f32[2,256]{1,0:T(2,128)S(1)} %broadcast_maximum_fusion, pred[2,1024]{1,0:T(4,128)(4,1)S(1)} %bitcast.42, f32[2,256]{1,0:T(2,128)S(1)} %fusion.5), kind=kOutput, calls=%fused_computation.18 | convolution fusion | flops 204144640 | bytes 3350528 | tf_op jit(solution)/shard_map/srk,skd->srd/dot_general | solution.py:36
  85.2 0.1 copy.25
  85.3 0.3 reshape.42
  85.6 0.6 multiply_reduce_fusion
  86.2 0.2 multiply_convert_fusion
  86.4 3.4 %fusion.31 = bf16[64,1536]{1,0:T(8,128)(2,1)S(1)} fusion(bf16[1536,1536]{1,0:T(8,128)(2,1)} %param.17, bf16[2,64,1536]{2,1,0:T(8,128)(2,1)S(1)} %multiply_convert_fusion, f32[1536]{0:T(1024)S(1)} %copy-done.1), kind=kOutput, calls=%fused_computation.42 | convolution fusion | flops 302776320 | bytes 5120000 | tf_op jit(solution)/shard_map/dot_general | solution.py:100
  89.8 4.7 %add_multiply_fusion = f32[64,1536]{1,0:T(8,128)} fusion(bf16[1536,1536]{1,0:T(8,128)(2,1)} %gather_fusion, bf16[64,1536]{1,0:T(8,128)(2,1)S(1)} %fusion.31, bf16[2,64,1536]{2,1,0:T(8,128)(2,1)S(1)} %multiply_convert_fusion, f32[1536]{0:T(1024)S(1)} %gather_fusion.1), kind=kOutput, calls=%fused_computation.48 | convolution fusion | flops 303169536 | bytes 5513216 | tf_op jit(solution)/shard_map/dot_general | solution.py:103
  (31 shorter events, 0.1 us)
Async XLA Ops:
  6.5 79.1 %copy-start = (bf16[768,1536]{1,0:T(8,128)(2,1)S(1)}, bf16[768,1536]{1,0:T(8,128)(2,1)}, u32[]{:S(2)}) copy-start(bf16[768,1536]{1,0:T(8,128)(2,1)} %param.15) | copy-start | bytes 7077892
  6.5 5.7 %copy-start.2 = (bf16[2,64,1536]{2,1,0:T(8,128)(2,1)S(1)}, bf16[2,64,1536]{2,1,0:T(8,128)(2,1)}, u32[]{:S(2)}) copy-start(bf16[2,64,1536]{2,1,0:T(8,128)(2,1)} %param.10) | copy-start | bytes 1179652
  6.5 10.2 %copy-start.7 = (s32[2,64]{1,0:T(2,128)S(1)}, s32[2,64]{1,0:T(2,128)}, u32[]{:S(2)}) copy-start(s32[2,64]{1,0:T(2,128)} %param.11) | copy-start | bytes 1540
  6.5 30.9 %copy-start.4 = (s32[1536]{0:T(1024)S(1)}, s32[1536]{0:T(1024)}, u32[]{:S(2)}) copy-start(s32[1536]{0:T(1024)} %param.19) | copy-start | bytes 18436
  6.5 74.8 %all-gather.3.cloned.1.call-start = ((), (), s32[]{:S(2)}) async-start(), calls=%async_computation | async-start | bytes 1671168 | tf_op jit(solution)/shard_map/all_gather | solution.py:86
  9.8 45.9 %copy-start.3 = (bf16[2,64,1536]{2,1,0:T(8,128)(2,1)}, bf16[2,64,1536]{2,1,0:T(8,128)(2,1)S(1)}, u32[]{:S(2)}) copy-start(bf16[2,64,1536]{2,1,0:T(8,128)(2,1)S(1)} %fusion.27) | copy-start | bytes 1179652
  12.3 1.6 %collective-permute-start = (bf16[64,1536]{1,0:T(8,128)(2,1)S(1)}, bf16[64,1536]{1,0:T(8,128)(2,1)S(1)}, u32[]{:S(2)}, u32[]{:S(2)}) collective-permute-start(bf16[64,1536]{1,0:T(8,128)(2,1)S(1)} %get-tuple-element.6), channel_id=1, source_target_pairs={{0,1},{1,0},{2,3},{3,2},{4,5},{5,4},{6,7},{7,6},{8,9},{9,8},{10,11... | collective-permute-start | bytes 589832 | tf_op jit(solution)/shard_map/ppermute | solution.py:11
  13.9 23.5 %collective-permute-start.1 = (bf16[64,1536]{1,0:T(8,128)(2,1)S(1)}, bf16[64,1536]{1,0:T(8,128)(2,1)S(1)}, u32[]{:S(2)}, u32[]{:S(2)}) collective-permute-start(bf16[64,1536]{1,0:T(8,128)(2,1)S(1)} %collective-permute-done), channel_id=1, source_target_pairs={{0,2},{1,3},{2,0},{3,1},{4,6},{5,7},{6,4},{7,5},{8,10},{9,11},{10,... | collective-permute-start | bytes 589832 | tf_op jit(solution)/shard_map/ppermute | solution.py:11
  37.4 11.5 %collective-permute-start.2 = (bf16[64,1536]{1,0:T(8,128)(2,1)S(1)}, bf16[64,1536]{1,0:T(8,128)(2,1)}, u32[]{:S(2)}, u32[]{:S(2)}) collective-permute-start(bf16[64,1536]{1,0:T(8,128)(2,1)S(1)} %collective-permute-done.1), channel_id=1, source_target_pairs={{0,4},{1,5},{2,6},{3,7},{4,0},{5,1},{6,2},{7,3},{8,12},{9,13},{10,... | collective-permute-start | bytes 589832 | tf_op jit(solution)/shard_map/ppermute | solution.py:11
  48.9 28.7 %collective-permute-start.3 = (bf16[64,1536]{1,0:T(8,128)(2,1)}, bf16[64,1536]{1,0:T(8,128)(2,1)S(1)}, u32[]{:S(2)}, u32[]{:S(2)}) collective-permute-start(bf16[64,1536]{1,0:T(8,128)(2,1)} %collective-permute-done.2), channel_id=1, source_target_pairs={{0,8},{1,9},{2,10},{3,11},{4,12},{5,13},{6,14},{7,15},{8,0},{9,1},... | collective-permute-start | bytes 589832 | tf_op jit(solution)/shard_map/ppermute | solution.py:11
  48.9 6.8 %copy-start.5 = (bf16[1536]{0:T(1024)(128)(2,1)S(1)}, bf16[1536]{0:T(1024)(128)(2,1)}, u32[]{:S(2)}) copy-start(bf16[1536]{0:T(1024)(128)(2,1)} %param.16) | copy-start | bytes 9220
  55.8 13.4 %copy-start.1 = (f32[1536]{0:T(1024)S(1)}, f32[1536]{0:T(1024)}, u32[]{:S(2)}) copy-start(f32[1536]{0:T(1024)} %param.18) | copy-start | bytes 18436
  69.2 9.0 %slice-start = ((bf16[2,64,1536]{2,1,0:T(8,128)(2,1)}), bf16[1,64,1536]{2,1,0:T(8,128)(2,1)S(1)}, s32[]{:S(2)}) async-start(bf16[2,64,1536]{2,1,0:T(8,128)(2,1)} %copy-done.3), calls=%async_computation.1 | async-start | bytes 393216 | tf_op jit(solution)/shard_map/slice | solution.py:71
  81.3 2.7 %copy-start.6 = (bf16[2,1024,384]{2,1,0:T(8,128)(2,1)S(1)}, bf16[2,1024,384]{2,1,0:T(8,128)(2,1)}, u32[]{:S(2)}) copy-start(bf16[2,1024,384]{2,1,0:T(8,128)(2,1)} %all-gather.3.cloned.1.call-done) | copy-start | bytes 4718596
Sparse Core Ops, SparseCore 0:
  12.3 45.7 all-gather.2
where the time goes:
time: 102 us; the launch traced here: 101 us
  local copies, waits for them, and re-layouts  30.3 us (30%)
  blocking collectives  20.7 us (20%)
  matrix products  16.5 us (16%)
  between operations  13.6 us (13%)
  waiting for transfers between devices  12.6 us (12%)
  other arithmetic  4.27 us (4%)
  starting transfers between devices  3.44 us (3%)
    all_gather x1, blocking collectives, per_device(): lax.all_gather(usable_flag, 'tok', axis=1, tiled=True)  20.7 us
    gather x1, local copies, waits for them, and re-layouts, per_device(): head_weight[:, track_perm]  13.4 us
    ppermute x4, waiting for transfers between devices, swapped(): return lax.ppermute(value, axis, pairs)  12.5 us
    gather x1, local copies, waits for them, and re-layouts, per_device(): head_bias[track_perm]  8.38 us
    unnamed x17, local copies, waits for them, and re-layouts  6.77 us
    dot_general x1, matrix products, per_device(): jnp.dot(normed_out[1], head_weight[:, track_perm], preferred_element_type...  4.69 us
    dot_general x1, matrix products, per_device(): jnp.dot(normed_out[0], head_weight, preferred_element_type=jnp.float32)  3.42 us
    ppermute x4, starting transfers between devices, swapped(): return lax.ppermute(value, axis, pairs)  3.41 us
  transfers between devices with their start and end apart: 5, of which 2 were waited for; matrix products, arithmetic and copies ran while one was open for 32% of the time, Pallas kernels for 0%

commit v1 on v0

--- a/solution.py
+++ b/solution.py
@@ -3,6 +3,18 @@
 import jax.numpy as jnp
 from jax import lax
 from jax.sharding import PartitionSpec as P
+
+
+def gather_around(value, axis, dim):
+    ways, here, step = (lax.axis_size(axis), lax.axis_index(axis), value.shape[dim])
+    shape = [n * ways if d == dim else n for d, n in enumerate(value.shape)]
+    full = lax.dynamic_update_slice_in_dim(
+        jnp.zeros(shape, value.dtype), value, here * step, axis=dim
+    )
+    for far in range(1, ways):
+        value = lax.ppermute(value, axis, [(d, (d + 1) % ways) for d in range(ways)])
+        full = lax.dynamic_update_slice_in_dim(full, value, (here - far) % ways * step, axis=dim)
+    return full
 
 
 def swapped(value, axis, distance):
@@ -84,7 +96,7 @@
         start_state,
         queries,
         lax.all_gather(key_value, "tok", axis=1, tiled=True),
-        lax.all_gather(usable_flag, "tok", axis=1, tiled=True),
+        gather_around(usable_flag, "tok", 1),
     )
     maxima, totals, accumulated = softmax_state
     attended = (

time: 102 us -> 154 us (1.51)
  waiting for transfers between devices: 12.6 us -> 80.4 us
  blocking collectives: 20.7 us -> 0 us
  local copies, waits for them, and re-layouts: 30.3 us -> 33.2 us
  starting transfers between devices: 3.44 us -> 5.25 us
    ppermute x0 -> x15, waiting for transfers between devices: none -> 67.1 us  [gather_around(): lax.ppermute(value, axis, [(d, (d + 1) % ways) for d in range(ways)])]
    all_gather x1 -> x0, blocking collectives: 20.7 us -> none  [per_device(): lax.all_gather(usable_flag, 'tok', axis=1, tiled=True)]
    dynamic_update_slice x0 -> x16, local copies, waits for them, and re-layouts: none -> 2.98 us  [the longest x15 2.82 us: gather_around(): lax.dynamic_update_slice_in_dim(full, value, (here - far) % ways * step,...]
    ppermute x4, starting transfers between devices: 3.41 us -> 5.04 us  [swapped(): return lax.ppermute(value, axis, pairs)]
  transfers between devices with their start and end apart: 5 -> 20, of which waited for: 2 -> 15; matrix products, arithmetic and copies ran while one was open for 32% -> 23% of each run, Pallas kernels for 0% -> 0%
where the time goes in v1:
time: 154 us
  waiting for transfers between devices  80.4 us (52%)
  local copies, waits for them, and re-layouts  33.2 us (22%)
  matrix products  16.5 us (11%)
  between operations  13.7 us (9%)
  starting transfers between devices  5.25 us (3%)
  other arithmetic  4.95 us (3%)
    ppermute x15, waiting for transfers between devices, gather_around(): lax.ppermute(value, axis, [(d, (d + 1) % ways) for d in range(ways)])  67.1 us
    gather x1, local copies, waits for them, and re-layouts, per_device(): head_weight[:, track_perm]  13.3 us
    ppermute x4, waiting for transfers between devices, swapped(): return lax.ppermute(value, axis, pairs)  13.3 us
    gather x1, local copies, waits for them, and re-layouts, per_device(): head_bias[track_perm]  8.38 us
    unnamed x17, local copies, waits for them, and re-layouts  6.77 us
    ppermute x4, starting transfers between devices, swapped(): return lax.ppermute(value, axis, pairs)  5.04 us
    dot_general x1, matrix products, per_device(): jnp.dot(normed_out[1], head_weight[:, track_perm], preferred_element_type...  4.69 us
    dot_general x1, matrix products, per_device(): jnp.dot(normed_out[0], head_weight, preferred_element_type=jnp.float32)  3.42 us
  transfers between devices with their start and end apart: 20, of which 15 were waited for; matrix products, arithmetic and copies ran while one was open for 23% of the time, Pallas kernels for 0%

profile of v1, /device:TPU:0, one launch (start us, length us, event | category | flops | bytes accessed | tf_op | source)
XLA Modules:
  0.0 153.9 jit_solution(3906463291871808619)
XLA Ops:
  6.6 0.8 convert_element_type.55
  7.4 1.2 fusion.25
  8.6 1.2 fusion.27
  9.8 2.4 %fusion.13 = bf16[2,64,384]{2,1,0:T(8,128)(2,1)} fusion(bf16[2,64,1536]{2,1,0:T(8,128)(2,1)S(1)} %fusion.27, bf16[1536,384]{1,0:T(8,128)(2,1)} %param.14), kind=kOutput, calls=%fused_computation.20 | convolution fusion | flops 151044096 | bytes 1671168 | tf_op jit(solution)/shard_map/std,de->ste/dot_general | solution.py:75
  12.9 1.0 collective-permute-done
  13.9 2.8 %collective-permute-start.1 = (bf16[64,1536]{1,0:T(8,128)(2,1)S(1)}, bf16[64,1536]{1,0:T(8,128)(2,1)S(1)}, u32[]{:S(2)}, u32[]{:S(2)}) collective-permute-start(bf16[64,1536]{1,0:T(8,128)(2,1)S(1)} %collective-permute-done), channel_id=1, source_target_pairs={{0,2},{1,3},{2,0},{3,1},{4,6},{5,7},{6,4},{7,5},{8,10},{9,11},{10,... | collective-permute-start | bytes 589832 | tf_op jit(solution)/shard_map/ppermute | solution.py:23
  16.7 5.6 %collective-permute-done.1 = bf16[64,1536]{1,0:T(8,128)(2,1)S(1)} collective-permute-done((bf16[64,1536]{1,0:T(8,128)(2,1)S(1)}, bf16[64,1536]{1,0:T(8,128)(2,1)S(1)}, u32[]{:S(2)}, u32[]{:S(2)}) %collective-permute-start.1) | collective-permute-done | bytes 196640 | tf_op jit(solution)/shard_map/ppermute | solution.py:23
  22.3 1.6 %collective-permute-start.2 = (bf16[64,1536]{1,0:T(8,128)(2,1)S(1)}, bf16[64,1536]{1,0:T(8,128)(2,1)}, u32[]{:S(2)}, u32[]{:S(2)}) collective-permute-start(bf16[64,1536]{1,0:T(8,128)(2,1)S(1)} %collective-permute-done.1), channel_id=1, source_target_pairs={{0,4},{1,5},{2,6},{3,7},{4,0},{5,1},{6,2},{7,3},{8,12},{9,13},{10,... | collective-permute-start | bytes 589832 | tf_op jit(solution)/shard_map/ppermute | solution.py:23
  23.9 0.7 fusion.47
  24.6 7.4 %collective-permute-done.5 = bf16[2,64]{1,0:T(2,128)(2,1)S(1)} collective-permute-done((bf16[2,64]{1,0:T(2,128)(2,1)S(1)}, bf16[2,64]{1,0:T(2,128)(2,1)S(1)}, u32[]{:S(2)}, u32[]{:S(2)}) %collective-permute-start.5) | collective-permute-done | bytes 288 | tf_op jit(solution)/shard_map/ppermute | solution.py:15
  32.0 5.7 %collective-permute-done.6 = bf16[2,64]{1,0:T(2,128)(2,1)S(1)} collective-permute-done((bf16[2,64]{1,0:T(2,128)(2,1)S(1)}, bf16[2,64]{1,0:T(2,128)(2,1)S(1)}, u32[]{:S(2)}, u32[]{:S(2)}) %collective-permute-start.6) | collective-permute-done | bytes 288 | tf_op jit(solution)/shard_map/ppermute | solution.py:15
  37.7 5.7 %collective-permute-done.7 = bf16[2,64]{1,0:T(2,128)(2,1)S(1)} collective-permute-done((bf16[2,64]{1,0:T(2,128)(2,1)S(1)}, bf16[2,64]{1,0:T(2,128)(2,1)S(1)}, u32[]{:S(2)}, u32[]{:S(2)}) %collective-permute-start.7) | collective-permute-done | bytes 288 | tf_op jit(solution)/shard_map/ppermute | solution.py:15
  43.4 5.7 %collective-permute-done.8 = bf16[2,64]{1,0:T(2,128)(2,1)S(1)} collective-permute-done((bf16[2,64]{1,0:T(2,128)(2,1)S(1)}, bf16[2,64]{1,0:T(2,128)(2,1)S(1)}, u32[]{:S(2)}, u32[]{:S(2)}) %collective-permute-start.8) | collective-permute-done | bytes 288 | tf_op jit(solution)/shard_map/ppermute | solution.py:15
  49.1 6.7 %copy.19 = bf16[1536,1536]{0,1:T(8,128)(2,1)} copy(bf16[1536,1536]{1,0:T(8,128)(2,1)} %param.17) | data formatting | bytes 9437184 | tf_op args[7]
  55.8 13.3 %gather_fusion = bf16[1536,1536]{1,0:T(8,128)(2,1)} fusion(bf16[1536,1536]{0,1:T(8,128)(2,1)} %copy.19, s32[2048]{0:T(1024)S(1)} %pad_clamp_fusion), kind=kCustom, calls=%fused_computation | custom fusion | bytes 9443328 | tf_op jit(solution)/shard_map/gather | solution.py:115
  69.2 8.4 %gather_fusion.1 = f32[1536]{0:T(1024)S(1)} fusion(f32[1536]{0:T(1024)S(1)} %copy-done.1, s32[2048]{0:T(1024)S(1)} %pad_clamp_fusion), kind=kCustom, calls=%fused_computation.1 | custom fusion | bytes 18432 | tf_op jit(solution)/shard_map/gather | solution.py:116
  77.7 5.6 %collective-permute-done.11 = bf16[2,64]{1,0:T(2,128)(2,1)S(1)} collective-permute-done((bf16[2,64]{1,0:T(2,128)(2,1)S(1)}, bf16[2,64]{1,0:T(2,128)(2,1)S(1)}, u32[]{:S(2)}, u32[]{:S(2)}) %collective-permute-start.11) | collective-permute-done | bytes 288 | tf_op jit(solution)/shard_map/ppermute | solution.py:15
  83.3 5.7 %collective-permute-done.12 = bf16[2,64]{1,0:T(2,128)(2,1)S(1)} collective-permute-done((bf16[2,64]{1,0:T(2,128)(2,1)S(1)}, bf16[2,64]{1,0:T(2,128)(2,1)S(1)}, u32[]{:S(2)}, u32[]{:S(2)}) %collective-permute-start.12) | collective-permute-done | bytes 288 | tf_op jit(solution)/shard_map/ppermute | solution.py:15
  89.0 5.7 %collective-permute-done.13 = bf16[2,64]{1,0:T(2,128)(2,1)S(1)} collective-permute-done((bf16[2,64]{1,0:T(2,128)(2,1)S(1)}, bf16[2,64]{1,0:T(2,128)(2,1)S(1)}, u32[]{:S(2)}, u32[]{:S(2)}) %collective-permute-start.13) | collective-permute-done | bytes 288 | tf_op jit(solution)/shard_map/ppermute | solution.py:15
  95.3 5.1 %collective-permute-done.14 = bf16[2,64]{1,0:T(2,128)(2,1)S(1)} collective-permute-done((bf16[2,64]{1,0:T(2,128)(2,1)S(1)}, bf16[2,64]{1,0:T(2,128)(2,1)S(1)}, u32[]{:S(2)}, u32[]{:S(2)}) %collective-permute-start.14) | collective-permute-done | bytes 288 | tf_op jit(solution)/shard_map/ppermute | solution.py:15
  101.0 5.1 %collective-permute-done.15 = bf16[2,64]{1,0:T(2,128)(2,1)S(1)} collective-permute-done((bf16[2,64]{1,0:T(2,128)(2,1)S(1)}, bf16[2,64]{1,0:T(2,128)(2,1)S(1)}, u32[]{:S(2)}, u32[]{:S(2)}) %collective-permute-start.15) | collective-permute-done | bytes 288 | tf_op jit(solution)/shard_map/ppermute | solution.py:15
  106.6 5.2 %collective-permute-done.16 = bf16[2,64]{1,0:T(2,128)(2,1)S(1)} collective-permute-done((bf16[2,64]{1,0:T(2,128)(2,1)S(1)}, bf16[2,64]{1,0:T(2,128)(2,1)S(1)}, u32[]{:S(2)}, u32[]{:S(2)}) %collective-permute-start.16) | collective-permute-done | bytes 288 | tf_op jit(solution)/shard_map/ppermute | solution.py:15
  112.4 5.1 %collective-permute-done.17 = bf16[2,64]{1,0:T(2,128)(2,1)S(1)} collective-permute-done((bf16[2,64]{1,0:T(2,128)(2,1)S(1)}, bf16[2,64]{1,0:T(2,128)(2,1)S(1)}, u32[]{:S(2)}, u32[]{:S(2)}) %collective-permute-start.17) | collective-permute-done | bytes 288 | tf_op jit(solution)/shard_map/ppermute | solution.py:15
  118.0 5.2 %collective-permute-done.18 = bf16[2,64]{1,0:T(2,128)(2,1)S(1)} collective-permute-done((bf16[2,64]{1,0:T(2,128)(2,1)S(1)}, bf16[2,64]{1,0:T(2,128)(2,1)S(1)}, u32[]{:S(2)}, u32[]{:S(2)}) %collective-permute-start.18) | collective-permute-done | bytes 288 | tf_op jit(solution)/shard_map/ppermute | solution.py:15
  123.5 6.7 %collective-permute-done.3 = bf16[64,1536]{1,0:T(8,128)(2,1)S(1)} collective-permute-done((bf16[64,1536]{1,0:T(8,128)(2,1)}, bf16[64,1536]{1,0:T(8,128)(2,1)S(1)}, u32[]{:S(2)}, u32[]{:S(2)}) %collective-permute-start.3) | collective-permute-done | bytes 196640 | tf_op jit(solution)/shard_map/ppermute | solution.py:23
  130.8 2.2 %fusion.10 = bf16[2,64,768]{2,1,0:T(8,128)(2,1)S(1)} fusion(bf16[1536,768]{1,0:T(8,128)(2,1)} %param.13, bf16[1,64,1536]{2,1,0:T(8,128)(2,1)S(1)} %fusion.36, bf16[1,64,1536]{2,1,0:T(8,128)(2,1)S(1)} %slice-done), kind=kOutput, calls=%fused_computation.19 | convolution fusion | flops 302284800 | bytes 2949120 | tf_op jit(solution)/shard_map/std,de->ste/dot_general | solution.py:85
  133.0 1.0 reshape.71
  134.0 2.0 %fusion.4 = (f32[2,256]{1,0:T(2,128)S(1)}, f32[2,256,1024]{2,1,0:T(8,128)S(1)}) fusion(pred[2,1024]{1,0:T(4,128)(4,1)S(1)} %compare_bitcast_fusion, bf16[2,256,192]{2,1,0:T(8,128)(2,1)} %reshape.71, bf16[2,1024,384]{2,1,0:T(8,128)(2,1)} %all-gather.2.cloned.1.call-done), kind=kOutput, calls=%fused_computation.10 | convolution fusion | flops 202898944 | bytes 3411968 | tf_op jit(solution)/shard_map/srd,skd->srk/dot_general | solution.py:40
  136.0 0.6 fusion.5
  136.6 1.2 fusion.9
  139.0 3.4 %fusion.31 = bf16[64,1536]{1,0:T(8,128)(2,1)S(1)} fusion(bf16[1536,1536]{1,0:T(8,128)(2,1)} %param.17, bf16[2,64,1536]{2,1,0:T(8,128)(2,1)S(1)} %multiply_convert_fusion, f32[1536]{0:T(1024)S(1)} %copy-done.1), kind=kOutput, calls=%fused_computation.42 | convolution fusion | flops 302776320 | bytes 5120000 | tf_op jit(solution)/shard_map/dot_general | solution.py:112
  142.4 4.7 %add_multiply_fusion = f32[64,1536]{1,0:T(8,128)} fusion(bf16[1536,1536]{1,0:T(8,128)(2,1)} %gather_fusion, bf16[64,1536]{1,0:T(8,128)(2,1)S(1)} %fusion.31, bf16[2,64,1536]{2,1,0:T(8,128)(2,1)S(1)} %multiply_convert_fusion, f32[1536]{0:T(1024)S(1)} %gather_fusion.1), kind=kOutput, calls=%fused_computation.48 | convolution fusion | flops 303169536 | bytes 5513216 | tf_op jit(solution)/shard_map/dot_general | solution.py:115
  (76 shorter events, 5.7 us)
Async XLA Ops:
  6.5 131.7 %copy-start = (bf16[768,1536]{1,0:T(8,128)(2,1)S(1)}, bf16[768,1536]{1,0:T(8,128)(2,1)}, u32[]{:S(2)}) copy-start(bf16[768,1536]{1,0:T(8,128)(2,1)} %param.15) | copy-start | bytes 7077892
  6.5 5.7 %copy-start.2 = (bf16[2,64,1536]{2,1,0:T(8,128)(2,1)S(1)}, bf16[2,64,1536]{2,1,0:T(8,128)(2,1)}, u32[]{:S(2)}) copy-start(bf16[2,64,1536]{2,1,0:T(8,128)(2,1)} %param.10) | copy-start | bytes 1179652
  6.5 6.3 %copy-start.7 = (s32[2,64]{1,0:T(2,128)S(1)}, s32[2,64]{1,0:T(2,128)}, u32[]{:S(2)}) copy-start(s32[2,64]{1,0:T(2,128)} %param.11) | copy-start | bytes 1540
  6.5 10.2 %copy-start.4 = (s32[1536]{0:T(1024)S(1)}, s32[1536]{0:T(1024)}, u32[]{:S(2)}) copy-start(s32[1536]{0:T(1024)} %param.19) | copy-start | bytes 18436
  6.5 127.4 %all-gather.2.cloned.1.call-start = ((), (), s32[]{:S(2)}) async-start(), calls=%async_computation | async-start | bytes 1671168 | tf_op jit(solution)/shard_map/all_gather | solution.py:98
  9.8 46.0 %copy-start.3 = (bf16[2,64,1536]{2,1,0:T(8,128)(2,1)}, bf16[2,64,1536]{2,1,0:T(8,128)(2,1)S(1)}, u32[]{:S(2)}) copy-start(bf16[2,64,1536]{2,1,0:T(8,128)(2,1)S(1)} %fusion.27) | copy-start | bytes 1179652
  12.3 1.6 %collective-permute-start = (bf16[64,1536]{1,0:T(8,128)(2,1)S(1)}, bf16[64,1536]{1,0:T(8,128)(2,1)S(1)}, u32[]{:S(2)}, u32[]{:S(2)}) collective-permute-start(bf16[64,1536]{1,0:T(8,128)(2,1)S(1)} %get-tuple-element.6), channel_id=1, source_target_pairs={{0,1},{1,0},{2,3},{3,2},{4,5},{5,4},{6,7},{7,6},{8,9},{9,8},{10,11... | collective-permute-start | bytes 589832 | tf_op jit(solution)/shard_map/ppermute | solution.py:23
  12.8 11.7 %collective-permute-start.4 = (bf16[2,64]{1,0:T(2,128)(2,1)S(1)}, bf16[2,64]{1,0:T(2,128)(2,1)S(1)}, u32[]{:S(2)}, u32[]{:S(2)}) collective-permute-start(bf16[2,64]{1,0:T(2,128)(2,1)S(1)} %compare_convert_fusion), channel_id=1, source_target_pairs={{0,1},{1,2},{2,3},{3,4},{4,5},{5,6},{6,7},{7,8},{8,9},{9,10},{10,1... | collective-permute-start | bytes 776 | tf_op jit(solution)/shard_map/ppermute | solution.py:15
  13.9 8.4 %collective-permute-start.1 = (bf16[64,1536]{1,0:T(8,128)(2,1)S(1)}, bf16[64,1536]{1,0:T(8,128)(2,1)S(1)}, u32[]{:S(2)}, u32[]{:S(2)}) collective-permute-start(bf16[64,1536]{1,0:T(8,128)(2,1)S(1)} %collective-permute-done), channel_id=1, source_target_pairs={{0,2},{1,3},{2,0},{3,1},{4,6},{5,7},{6,4},{7,5},{8,10},{9,11},{10,... | collective-permute-start | bytes 589832 | tf_op jit(solution)/shard_map/ppermute | solution.py:23
  22.3 101.1 %collective-permute-start.2 = (bf16[64,1536]{1,0:T(8,128)(2,1)S(1)}, bf16[64,1536]{1,0:T(8,128)(2,1)}, u32[]{:S(2)}, u32[]{:S(2)}) collective-permute-start(bf16[64,1536]{1,0:T(8,128)(2,1)S(1)} %collective-permute-done.1), channel_id=1, source_target_pairs={{0,4},{1,5},{2,6},{3,7},{4,0},{5,1},{6,2},{7,3},{8,12},{9,13},{10,... | collective-permute-start | bytes 589832 | tf_op jit(solution)/shard_map/ppermute | solution.py:23
  24.6 7.4 %collective-permute-start.5 = (bf16[2,64]{1,0:T(2,128)(2,1)S(1)}, bf16[2,64]{1,0:T(2,128)(2,1)S(1)}, u32[]{:S(2)}, u32[]{:S(2)}) collective-permute-start(bf16[2,64]{1,0:T(2,128)(2,1)S(1)} %collective-permute-done.4), channel_id=1, source_target_pairs={{0,1},{1,2},{2,3},{3,4},{4,5},{5,6},{6,7},{7,8},{8,9},{9,10},{10,1... | collective-permute-start | bytes 776 | tf_op jit(solution)/shard_map/ppermute | solution.py:15
  32.0 5.7 %collective-permute-start.6 = (bf16[2,64]{1,0:T(2,128)(2,1)S(1)}, bf16[2,64]{1,0:T(2,128)(2,1)S(1)}, u32[]{:S(2)}, u32[]{:S(2)}) collective-permute-start(bf16[2,64]{1,0:T(2,128)(2,1)S(1)} %collective-permute-done.5), channel_id=1, source_target_pairs={{0,1},{1,2},{2,3},{3,4},{4,5},{5,6},{6,7},{7,8},{8,9},{9,10},{10,1... | collective-permute-start | bytes 776 | tf_op jit(solution)/shard_map/ppermute | solution.py:15
  37.6 5.7 %collective-permute-start.7 = (bf16[2,64]{1,0:T(2,128)(2,1)S(1)}, bf16[2,64]{1,0:T(2,128)(2,1)S(1)}, u32[]{:S(2)}, u32[]{:S(2)}) collective-permute-start(bf16[2,64]{1,0:T(2,128)(2,1)S(1)} %collective-permute-done.6), channel_id=1, source_target_pairs={{0,1},{1,2},{2,3},{3,4},{4,5},{5,6},{6,7},{7,8},{8,9},{9,10},{10,1... | collective-permute-start | bytes 776 | tf_op jit(solution)/shard_map/ppermute | solution.py:15
  43.3 5.7 %collective-permute-start.8 = (bf16[2,64]{1,0:T(2,128)(2,1)S(1)}, bf16[2,64]{1,0:T(2,128)(2,1)S(1)}, u32[]{:S(2)}, u32[]{:S(2)}) collective-permute-start(bf16[2,64]{1,0:T(2,128)(2,1)S(1)} %collective-permute-done.7), channel_id=1, source_target_pairs={{0,1},{1,2},{2,3},{3,4},{4,5},{5,6},{6,7},{7,8},{8,9},{9,10},{10,1... | collective-permute-start | bytes 776 | tf_op jit(solution)/shard_map/ppermute | solution.py:15
  49.0 6.8 %collective-permute-start.9 = (bf16[2,64]{1,0:T(2,128)(2,1)S(1)}, bf16[2,64]{1,0:T(2,128)(2,1)S(1)}, u32[]{:S(2)}, u32[]{:S(2)}) collective-permute-start(bf16[2,64]{1,0:T(2,128)(2,1)S(1)} %collective-permute-done.8), channel_id=1, source_target_pairs={{0,1},{1,2},{2,3},{3,4},{4,5},{5,6},{6,7},{7,8},{8,9},{9,10},{10,1... | collective-permute-start | bytes 776 | tf_op jit(solution)/shard_map/ppermute | solution.py:15
  49.1 6.8 %copy-start.5 = (bf16[1536]{0:T(1024)(128)(2,1)S(1)}, bf16[1536]{0:T(1024)(128)(2,1)}, u32[]{:S(2)}) copy-start(bf16[1536]{0:T(1024)(128)(2,1)} %param.16) | copy-start | bytes 9220
  55.8 21.8 %collective-permute-start.10 = (bf16[2,64]{1,0:T(2,128)(2,1)S(1)}, bf16[2,64]{1,0:T(2,128)(2,1)S(1)}, u32[]{:S(2)}, u32[]{:S(2)}) collective-permute-start(bf16[2,64]{1,0:T(2,128)(2,1)S(1)} %collective-permute-done.9), channel_id=1, source_target_pairs={{0,1},{1,2},{2,3},{3,4},{4,5},{5,6},{6,7},{7,8},{8,9},{9,10},{10,1... | collective-permute-start | bytes 776 | tf_op jit(solution)/shard_map/ppermute | solution.py:15
  55.8 13.4 %copy-start.1 = (f32[1536]{0:T(1024)S(1)}, f32[1536]{0:T(1024)}, u32[]{:S(2)}) copy-start(f32[1536]{0:T(1024)} %param.18) | copy-start | bytes 18436
  69.2 61.6 %slice-start = ((bf16[2,64,1536]{2,1,0:T(8,128)(2,1)}), bf16[1,64,1536]{2,1,0:T(8,128)(2,1)S(1)}, s32[]{:S(2)}) async-start(bf16[2,64,1536]{2,1,0:T(8,128)(2,1)} %copy-done.3), calls=%async_computation.1 | async-start | bytes 393216 | tf_op jit(solution)/shard_map/slice | solution.py:83
  77.6 5.7 %collective-permute-start.11 = (bf16[2,64]{1,0:T(2,128)(2,1)S(1)}, bf16[2,64]{1,0:T(2,128)(2,1)S(1)}, u32[]{:S(2)}, u32[]{:S(2)}) collective-permute-start(bf16[2,64]{1,0:T(2,128)(2,1)S(1)} %collective-permute-done.10), channel_id=1, source_target_pairs={{0,1},{1,2},{2,3},{3,4},{4,5},{5,6},{6,7},{7,8},{8,9},{9,10},{10,1... | collective-permute-start | bytes 776 | tf_op jit(solution)/shard_map/ppermute | solution.py:15
  83.3 5.7 %collective-permute-start.12 = (bf16[2,64]{1,0:T(2,128)(2,1)S(1)}, bf16[2,64]{1,0:T(2,128)(2,1)S(1)}, u32[]{:S(2)}, u32[]{:S(2)}) collective-permute-start(bf16[2,64]{1,0:T(2,128)(2,1)S(1)} %collective-permute-done.11), channel_id=1, source_target_pairs={{0,1},{1,2},{2,3},{3,4},{4,5},{5,6},{6,7},{7,8},{8,9},{9,10},{10,1... | collective-permute-start | bytes 776 | tf_op jit(solution)/shard_map/ppermute | solution.py:15
  89.0 5.7 %collective-permute-start.13 = (bf16[2,64]{1,0:T(2,128)(2,1)S(1)}, bf16[2,64]{1,0:T(2,128)(2,1)S(1)}, u32[]{:S(2)}, u32[]{:S(2)}) collective-permute-start(bf16[2,64]{1,0:T(2,128)(2,1)S(1)} %collective-permute-done.12), channel_id=1, source_target_pairs={{0,1},{1,2},{2,3},{3,4},{4,5},{5,6},{6,7},{7,8},{8,9},{9,10},{10,1... | collective-permute-start | bytes 776 | tf_op jit(solution)/shard_map/ppermute | solution.py:15
  94.7 5.7 %collective-permute-start.14 = (bf16[2,64]{1,0:T(2,128)(2,1)S(1)}, bf16[2,64]{1,0:T(2,128)(2,1)S(1)}, u32[]{:S(2)}, u32[]{:S(2)}) collective-permute-start(bf16[2,64]{1,0:T(2,128)(2,1)S(1)} %collective-permute-done.13), channel_id=1, source_target_pairs={{0,1},{1,2},{2,3},{3,4},{4,5},{5,6},{6,7},{7,8},{8,9},{9,10},{10,1... | collective-permute-start | bytes 776 | tf_op jit(solution)/shard_map/ppermute | solution.py:15
  100.4 5.7 %collective-permute-start.15 = (bf16[2,64]{1,0:T(2,128)(2,1)S(1)}, bf16[2,64]{1,0:T(2,128)(2,1)S(1)}, u32[]{:S(2)}, u32[]{:S(2)}) collective-permute-start(bf16[2,64]{1,0:T(2,128)(2,1)S(1)} %collective-permute-done.14), channel_id=1, source_target_pairs={{0,1},{1,2},{2,3},{3,4},{4,5},{5,6},{6,7},{7,8},{8,9},{9,10},{10,1... | collective-permute-start | bytes 776 | tf_op jit(solution)/shard_map/ppermute | solution.py:15
  106.1 5.7 %collective-permute-start.16 = (bf16[2,64]{1,0:T(2,128)(2,1)S(1)}, bf16[2,64]{1,0:T(2,128)(2,1)S(1)}, u32[]{:S(2)}, u32[]{:S(2)}) collective-permute-start(bf16[2,64]{1,0:T(2,128)(2,1)S(1)} %collective-permute-done.15), channel_id=1, source_target_pairs={{0,1},{1,2},{2,3},{3,4},{4,5},{5,6},{6,7},{7,8},{8,9},{9,10},{10,1... | collective-permute-start | bytes 776 | tf_op jit(solution)/shard_map/ppermute | solution.py:15
  111.8 5.7 %collective-permute-start.17 = (bf16[2,64]{1,0:T(2,128)(2,1)S(1)}, bf16[2,64]{1,0:T(2,128)(2,1)S(1)}, u32[]{:S(2)}, u32[]{:S(2)}) collective-permute-start(bf16[2,64]{1,0:T(2,128)(2,1)S(1)} %collective-permute-done.16), channel_id=1, source_target_pairs={{0,1},{1,2},{2,3},{3,4},{4,5},{5,6},{6,7},{7,8},{8,9},{9,10},{10,1... | collective-permute-start | bytes 776 | tf_op jit(solution)/shard_map/ppermute | solution.py:15
  117.5 5.7 %collective-permute-start.18 = (bf16[2,64]{1,0:T(2,128)(2,1)S(1)}, bf16[2,64]{1,0:T(2,128)(2,1)S(1)}, u32[]{:S(2)}, u32[]{:S(2)}) collective-permute-start(bf16[2,64]{1,0:T(2,128)(2,1)S(1)} %collective-permute-done.17), channel_id=1, source_target_pairs={{0,1},{1,2},{2,3},{3,4},{4,5},{5,6},{6,7},{7,8},{8,9},{9,10},{10,1... | collective-permute-start | bytes 776 | tf_op jit(solution)/shard_map/ppermute | solution.py:15
  123.4 6.8 %collective-permute-start.3 = (bf16[64,1536]{1,0:T(8,128)(2,1)}, bf16[64,1536]{1,0:T(8,128)(2,1)S(1)}, u32[]{:S(2)}, u32[]{:S(2)}) collective-permute-start(bf16[64,1536]{1,0:T(8,128)(2,1)} %collective-permute-done.2), channel_id=1, source_target_pairs={{0,8},{1,9},{2,10},{3,11},{4,12},{5,13},{6,14},{7,15},{8,0},{9,1},... | collective-permute-start | bytes 589832 | tf_op jit(solution)/shard_map/ppermute | solution.py:23
  134.0 2.7 %copy-start.6 = (bf16[2,1024,384]{2,1,0:T(8,128)(2,1)S(1)}, bf16[2,1024,384]{2,1,0:T(8,128)(2,1)}, u32[]{:S(2)}) copy-start(bf16[2,1024,384]{2,1,0:T(8,128)(2,1)} %all-gather.2.cloned.1.call-done) | copy-start | bytes 4718596
Sparse Core Ops, SparseCore 0:
  12.3 43.2 all-gather.1
